TPU v7x, 32 devices: a whole 2x2x4 slice. The times are simulated.
32 devices in a mesh: dp: 4 (over y, core), ctx: 8 (over z, x).
Axes of the slice: x: 2, y: 2, z: 4, core: 2. Of those that a mesh axis runs over, the one named last changes fastest.
Arguments:
- queries: bfloat16 [4608, 256], P(('dp', 'ctx')), parts along dimension 0, may hold values from -5 to 5
- keys: bfloat16 [4608, 256], P(('dp', 'ctx')), parts along dimension 0, may hold values from -5 to 5
- values: bfloat16 [4608, 256], P(('dp', 'ctx')), parts along dimension 0, may hold values from -2.5 to 2.5
- out_grad: bfloat16 [4608, 256], P(('dp', 'ctx')), parts along dimension 0, may hold values from -5 to 5
- span_end: int32 [4608], P(('dp', 'ctx')), parts along dimension 0, may hold values from 0 to 1152, as said below
Outputs:
- output: bfloat16 [4608, 256], P(('dp', 'ctx')), parts along dimension 0
- query_grad: float32 [4608, 256], P(('dp', 'ctx')), parts along dimension 0
- key_grad: float32 [4608, 256], P(('dp', 'ctx')), parts along dimension 0
- value_grad: float32 [4608, 256], P(('dp', 'ctx')), parts along dimension 0
There are 4 independent parts, one for each index of `dp`. A program takes and returns all parts, laid end to end along the dimension named above; each array names one. Nothing has to cross between parts.
Inputs may be any that keep to these rules, and one draw needn't show every extreme that they name: `span_end`: image spans are runs of consecutive tokens, each of at most 288 tokens; every token of a span holds the position just past the span's last token; the last 288 tokens of a document form one span.
All inputs are finite; a program needn't handle non-finite values.
Results may differ from a plain program's by a relative error of at most 0.035.
Values may be sent and summed in bfloat16 or wider, within the bound.
A program may use at most 64 MiB of HBM per device.

v0:
```python
import jax
import jax.numpy as jnp
from jax import lax
from jax.sharding import PartitionSpec as P

HEADS = 2
HEAD_DIM = 128


def split_heads(matrix):
    return matrix.reshape(matrix.shape[0], HEADS, HEAD_DIM)


def local(queries, keys, values, out_grad, span_end):
    row_count = queries.shape[0]
    scaling = HEAD_DIM ** (-0.5)
    device = lax.axis_index("ctx")
    base_positions = device * row_count + jnp.arange(row_count, dtype=jnp.int32)
    base_limits = jnp.maximum(base_positions + 1, span_end)
    limit_all = lax.all_gather(base_limits, "ctx", axis=0, tiled=True)
    query_rows_own, key_rows_own, value_rows_own, grad_rows_own = (queries, keys, values, out_grad)
    query_own = split_heads(query_rows_own)
    key_own = split_heads(key_rows_own)
    value_own = split_heads(value_rows_own)
    grad_own = split_heads(grad_rows_own)

    def own_scores(key_piece):
        columns = jnp.arange(key_piece.shape[0], dtype=jnp.int32)
        visible = (columns[None, :] < base_limits[:, None])[None]
        scores = (
            jnp.einsum("qhd,khd->hqk", query_own, key_piece, preferred_element_type=jnp.float32)
            * scaling
        )
        return (scores, visible)

    pieces = (
        lax.all_gather(keys, "ctx", axis=0, tiled=True),
        lax.all_gather(values, "ctx", axis=0, tiled=True),
    )
    run_high = jnp.full((HEADS, row_count), -1e30, jnp.float32)
    weighted = jnp.zeros((row_count, HEADS, HEAD_DIM), jnp.float32)
    key_piece = split_heads(pieces[0])
    value_piece = split_heads(pieces[1])
    scores, visible = own_scores(key_piece)
    scores = jnp.where(visible, scores, -1e30)
    new_high = jnp.maximum(run_high, jnp.max(scores, axis=-1))
    factor = jnp.exp(run_high - new_high)
    weights_now = jnp.where(visible, jnp.exp(scores - new_high[..., None]), 0.0)
    run_total = jnp.sum(weights_now, axis=-1)
    weighted = weighted * factor.T[:, :, None] + jnp.einsum(
        "hqk,khd->qhd",
        weights_now,
        value_piece.astype(jnp.float32),
        precision=lax.Precision.HIGHEST,
        preferred_element_type=jnp.float32,
    )
    run_high, run_total, weighted = (new_high, run_total, weighted)
    log_total = run_high + jnp.log(run_total)
    output = (weighted / run_total.T[:, :, None]).astype(jnp.bfloat16)
    row_dot = jnp.sum(grad_own.astype(jnp.float32) * output.astype(jnp.float32), axis=-1).T
    pieces = (
        lax.all_gather(keys, "ctx", axis=0, tiled=True),
        lax.all_gather(values, "ctx", axis=0, tiled=True),
    )
    key_piece = split_heads(pieces[0])
    value_piece = split_heads(pieces[1])
    scores, visible = own_scores(key_piece)
    probs = jnp.where(visible, jnp.exp(scores - log_total[..., None]), 0.0)
    prob_grad = jnp.einsum(
        "qhd,khd->hqk", grad_own, value_piece, preferred_element_type=jnp.float32
    )
    score_grad = probs * (prob_grad - row_dot[..., None])
    query_grad = jnp.einsum(
        "hqk,khd->qhd",
        score_grad.astype(jnp.bfloat16),
        key_piece,
        preferred_element_type=jnp.float32,
    )
    log_all, dot_all = (
        lax.all_gather(log_total, "ctx", axis=1, tiled=True),
        lax.all_gather(row_dot, "ctx", axis=1, tiled=True),
    )
    pieces = (
        lax.all_gather(queries, "ctx", axis=0, tiled=True),
        lax.all_gather(out_grad, "ctx", axis=0, tiled=True),
    )
    query_piece = split_heads(pieces[0])
    grad_piece = split_heads(pieces[1])
    visible = (base_positions[None, :] < limit_all[:, None])[None]
    scores = (
        jnp.einsum("qhd,khd->hqk", query_piece, key_own, preferred_element_type=jnp.float32)
        * scaling
    )
    probs = jnp.where(visible, jnp.exp(scores - log_all[..., None]), 0.0)
    value_grad = jnp.einsum(
        "hqk,qhd->khd", probs.astype(jnp.bfloat16), grad_piece, preferred_element_type=jnp.float32
    )
    prob_grad = jnp.einsum(
        "qhd,khd->hqk", grad_piece, value_own, preferred_element_type=jnp.float32
    )
    score_grad = probs * (prob_grad - dot_all[..., None])
    key_grad = jnp.einsum(
        "hqk,qhd->khd",
        score_grad.astype(jnp.bfloat16),
        query_piece,
        preferred_element_type=jnp.float32,
    )
    key_grad, value_grad = (key_grad, value_grad)
    flat_shape = (row_count, HEADS * HEAD_DIM)
    results = (
        output.astype(jnp.float32).reshape(flat_shape),
        (query_grad * scaling).reshape(flat_shape),
        (key_grad * scaling).reshape(flat_shape),
        value_grad.reshape(flat_shape),
    )
    return (results[0].astype(jnp.bfloat16), results[1], results[2], results[3])


def solution(mesh):
    in_specs = (
        P(("dp", "ctx"), None),
        P(("dp", "ctx"), None),
        P(("dp", "ctx"), None),
        P(("dp", "ctx"), None),
        P(("dp", "ctx")),
    )
    out_specs = (
        P(("dp", "ctx"), None),
        P(("dp", "ctx"), None),
        P(("dp", "ctx"), None),
        P(("dp", "ctx"), None),
    )
    return jax.shard_map(local, mesh=mesh, in_specs=in_specs, out_specs=out_specs, check_vma=False)
```

profile of v0, /device:TPU:0, one launch (start us, length us, event | category | flops | bytes accessed | tf_op | source)
XLA Modules:
  0.0 201.7 jit_solution(14404172331278344812)
XLA Ops:
  0.6 1.3 dynamic-slice
  2.6 0.8 fusion.42
  3.6 33.4 %all_gather.23 = bf16[1152,256]{1,0:T(8,128)(2,1)S(1)} all-gather(bf16[144,256]{1,0:T(8,128)(2,1)} %param.6), channel_id=1, replica_groups=mesh['dp'=4,'ctx'=8] {'ctx'}, dimensions={0}, use_global_device_ids=true | all-gather | bytes 663552 | tf_op jit(solution)/shard_map/all_gather | solution.py:37
  37.0 0.3 copy.28
  37.3 0.5 select_reduce_fusion
  37.8 0.5 fusion.16
  38.3 31.5 %all_gather.24 = bf16[1152,256]{1,0:T(8,128)(2,1)S(1)} all-gather(bf16[144,256]{1,0:T(8,128)(2,1)S(1)} %copy-done.1), channel_id=1, replica_groups=mesh['dp'=4,'ctx'=8] {'ctx'}, dimensions={0}, use_global_device_ids=true | all-gather | bytes 663552 | tf_op jit(solution)/shard_map/all_gather | solution.py:38
  69.8 0.3 copy.31
  70.1 1.2 multiply_reduce_fusion
  71.4 0.6 copy_bitcast_fusion.3
  72.0 0.7 fusion.10
  72.8 0.7 copy.92
  73.4 31.7 %all_gather.28 = bf16[1152,256]{1,0:T(8,128)(2,1)S(1)} all-gather(bf16[144,256]{1,0:T(8,128)(2,1)S(1)} %copy-done.2), channel_id=1, replica_groups=mesh['dp'=4,'ctx'=8] {'ctx'}, dimensions={0}, use_global_device_ids=true | all-gather | bytes 663552 | tf_op jit(solution)/shard_map/all_gather | solution.py:85
  105.1 0.3 copy.43
  105.4 31.4 %all_gather.26 = bf16[1152,256]{1,0:T(8,128)(2,1)S(1)} all-gather(bf16[144,256]{1,0:T(8,128)(2,1)S(1)} %copy-done), channel_id=1, replica_groups=mesh['dp'=4,'ctx'=8] {'ctx'}, dimensions={0}, use_global_device_ids=true | all-gather | bytes 663552 | tf_op jit(solution)/shard_map/all_gather | solution.py:84
  136.8 0.3 copy.39
  137.1 26.1 %all-gather = f32[8,144,2]{1,2,0:T(2,128)S(1)} all-gather(f32[1,144,2]{1,2,0:T(2,128)S(1)} %bitcast.105), channel_id=1, replica_groups=mesh['dp'=4,'ctx'=8] {'ctx'}, dimensions={0}, use_global_device_ids=true | all-gather | bytes 10368 | tf_op jit(solution)/shard_map/all_gather | solution.py:80
  163.3 9.9 %all-reduce = s32[1152]{0:T(1024)S(1)} all-reduce(s32[1152]{0:T(1024)S(1)} %get-tuple-element.4), channel_id=1, replica_groups=mesh['dp'=4,'ctx'=8] {'ctx'}, use_global_device_ids=true, to_apply=%add | all-reduce | flops 1152 | bytes 9216
  173.2 0.2 broadcast_compare_fusion
  173.4 0.5 fusion.4
  173.9 0.3 convolution_bitcast_fusion
  174.3 26.1 %all-gather.1 = f32[8,144,2]{1,2,0:T(2,128)S(1)} all-gather(f32[1,144,2]{1,2,0:T(2,128)S(1)} %bitcast.107), channel_id=1, replica_groups=mesh['dp'=4,'ctx'=8] {'ctx'}, dimensions={0}, use_global_device_ids=true | all-gather | bytes 10368 | tf_op jit(solution)/shard_map/all_gather | solution.py:81
  200.5 0.5 fusion.12
  201.0 0.7 copy_bitcast_fusion
  (17 shorter events, 0.4 us)
Async XLA Ops:
  0.6 36.7 %copy-start = (bf16[144,256]{1,0:T(8,128)(2,1)S(1)}, bf16[144,256]{1,0:T(8,128)(2,1)}, u32[]{:S(2)}) copy-start(bf16[144,256]{1,0:T(8,128)(2,1)} %param.5) | copy-start | bytes 221188
  37.3 1.0 copy-start.1
  37.8 32.3 %copy-start.2 = (bf16[144,256]{1,0:T(8,128)(2,1)S(1)}, bf16[144,256]{1,0:T(8,128)(2,1)}, u32[]{:S(2)}) copy-start(bf16[144,256]{1,0:T(8,128)(2,1)} %param.8) | copy-start | bytes 221188
  105.4 68.0 %copy-start.3 = (bf16[144,256]{1,0:T(8,128)(2,1)S(1)}, bf16[144,256]{1,0:T(8,128)(2,1)}, u32[]{:S(2)}) copy-start(bf16[144,256]{1,0:T(8,128)(2,1)} %param.6) | copy-start | bytes 221188
where the time goes:
time: 202 us
  blocking collectives  190 us (94%)
  local copies, waits for them, and re-layouts  4.71 us (2%)
  matrix products  3.81 us (2%)
    all_gather x1, blocking collectives, local(): lax.all_gather(keys, 'ctx', axis=0, tiled=True)  33.4 us
    all_gather x1, blocking collectives, local(): lax.all_gather(out_grad, 'ctx', axis=0, tiled=True)  31.7 us
    all_gather x1, blocking collectives, local(): lax.all_gather(values, 'ctx', axis=0, tiled=True)  31.5 us
    all_gather x1, blocking collectives, local(): lax.all_gather(queries, 'ctx', axis=0, tiled=True)  31.4 us
    all_gather x1, blocking collectives, local(): lax.all_gather(log_total, 'ctx', axis=1, tiled=True)  26.1 us
    all_gather x1, blocking collectives, local(): lax.all_gather(row_dot, 'ctx', axis=1, tiled=True)  26.1 us
    unnamed x1, blocking collectives  9.9 us

commit v1 on v0

--- a/solution.py
+++ b/solution.py
@@ -5,6 +5,27 @@
 
 HEADS = 2
 HEAD_DIM = 128
+
+
+def sample_edit(body, group_axis):
+    known = lax.axis_size(group_axis)
+    frame_out = lax.axis_index(group_axis)
+    a_next, fresh, mixed_arr = (known, frame_out, body.shape[1])
+    z_new, b_now = (body, 1)
+    while b_now < a_next:
+        z_new = jnp.concatenate(
+            [
+                z_new,
+                lax.ppermute(
+                    z_new,
+                    axis_name=group_axis,
+                    perm=tuple(((h, (h - b_now) % a_next) for h in range(a_next))),
+                ),
+            ],
+            1,
+        )
+        b_now = 2 * b_now
+    return jnp.roll(z_new, fresh * mixed_arr, 1)
 
 
 def split_heads(matrix):
@@ -77,7 +98,7 @@
         preferred_element_type=jnp.float32,
     )
     log_all, dot_all = (
-        lax.all_gather(log_total, "ctx", axis=1, tiled=True),
+        sample_edit(log_total, "ctx"),
         lax.all_gather(row_dot, "ctx", axis=1, tiled=True),
     )
     pieces = (

time: 202 us -> 185 us (0.916)
  blocking collectives: 190 us -> 163 us
  starting transfers between devices: 0 us -> 4.98 us
  matrix products: 3.81 us -> 6.45 us
    all_gather x1 -> x0, blocking collectives: 26.1 us -> none  [local(): lax.all_gather(log_total, 'ctx', axis=1, tiled=True)]
    ppermute x0 -> x3, starting transfers between devices: none -> 4.98 us  [sample_edit(): lax.ppermute(z_new, axis_name=group_axis, perm=tuple(((h, (h - b_now) % a...]
  transfers between devices with their start and end apart: 0 -> 3, of which waited for: 0 -> 1; matrix products, arithmetic and copies ran while one was open for 0% -> 4% of each run, Pallas kernels for 0% -> 0%
where the time goes in v1:
time: 185 us
  blocking collectives  163 us (88%)
  matrix products  6.45 us (3%)
  local copies, waits for them, and re-layouts  5.61 us (3%)
  starting transfers between devices  4.98 us (3%)
    all_gather x1, blocking collectives, local(): lax.all_gather(keys, 'ctx', axis=0, tiled=True)  33.4 us
    all_gather x1, blocking collectives, local(): lax.all_gather(queries, 'ctx', axis=0, tiled=True)  31.6 us
    all_gather x1, blocking collectives, local(): lax.all_gather(values, 'ctx', axis=0, tiled=True)  31.5 us
    all_gather x1, blocking collectives, local(): lax.all_gather(out_grad, 'ctx', axis=0, tiled=True)  31.3 us
    all_gather x1, blocking collectives, local(): lax.all_gather(row_dot, 'ctx', axis=1, tiled=True)  26.2 us
    unnamed x1, blocking collectives  8.83 us
    ppermute x3, starting transfers between devices, sample_edit(): lax.ppermute(z_new, axis_name=group_axis, perm=tuple(((h, (h - b_now) % a...  4.98 us
  transfers between devices with their start and end apart: 3, of which 1 were waited for; matrix products, arithmetic and copies ran while one was open for 4% of the time, Pallas kernels for 0%

profile of v1, /device:TPU:0, one launch (start us, length us, event | category | flops | bytes accessed | tf_op | source)
XLA Modules:
  0.0 185.0 jit_solution(11761370676163984736)
XLA Ops:
  0.6 1.3 dynamic-slice
  2.6 0.8 fusion.48
  3.6 33.4 %all_gather.20 = bf16[1152,256]{1,0:T(8,128)(2,1)S(1)} all-gather(bf16[144,256]{1,0:T(8,128)(2,1)} %param.6), channel_id=1, replica_groups=mesh['dp'=4,'ctx'=8] {'ctx'}, dimensions={0}, use_global_device_ids=true | all-gather | bytes 663552 | tf_op jit(solution)/shard_map/all_gather | solution.py:58
  37.3 0.5 select_reduce_fusion
  37.8 0.5 fusion.14
  38.3 4.4 %collective-permute-start = (f32[2,144]{1,0:T(2,128)S(1)}, f32[2,144]{1,0:T(2,128)S(1)}, u32[]{:S(2)}, u32[]{:S(2)}) collective-permute-start(f32[2,144]{1,0:T(2,128)S(1)} %get-tuple-element.6), channel_id=1, source_target_pairs={{0,7},{1,0},{2,1},{3,2},{4,3},{5,4},{6,5},{7,6},{8,15},{9,8},{10,9... | collective-permute-start | bytes 3464 | tf_op jit(solution)/shard_map/ppermute | solution.py:19
  42.8 31.6 %all_gather.23 = bf16[1152,256]{1,0:T(8,128)(2,1)S(1)} all-gather(bf16[144,256]{1,0:T(8,128)(2,1)S(1)} %copy-done.1), channel_id=1, replica_groups=mesh['dp'=4,'ctx'=8] {'ctx'}, dimensions={0}, use_global_device_ids=true | all-gather | bytes 663552 | tf_op jit(solution)/shard_map/all_gather | solution.py:105
  74.4 31.5 %all_gather.21 = bf16[1152,256]{1,0:T(8,128)(2,1)S(1)} all-gather(bf16[144,256]{1,0:T(8,128)(2,1)S(1)} %copy-done.6), channel_id=1, replica_groups=mesh['dp'=4,'ctx'=8] {'ctx'}, dimensions={0}, use_global_device_ids=true | all-gather | bytes 663552 | tf_op jit(solution)/shard_map/all_gather | solution.py:59
  105.9 1.1 copy.31
  107.0 2.9 %multiply_reduce_fusion = (f32[144,2]{0,1:T(2,128)S(1)}, bf16[144,2,128]{2,0,1:T(8,128)(2,1)}) fusion(f32[144,2]{0,1:T(2,128)S(1)} %bitcast.97, bf16[1152,2,128]{0,2,1:T(8,128)(2,1)} %bitcast.93, f32[2,144,1152]{2,1,0:T(8,128)S(1)} %get-tuple-element.9, f32[2,144]{1,0:T(2,128)S(1)} %broadcast_maximum_fusion, pred[144,1152]{1,0:T(8,128)(4,1)S(1)} %iota_compare_fusion, ...), kind=kOutput, calls=%fused_computation.44 | convolution fusion | flops 510861024 | bytes 2234880 | tf_op jit(solution)/shard_map/hqk,khd->qhd/dot_general | solution.py:71
  109.8 1.7 fusion.7
  111.5 0.3 copy.39
  111.8 0.3 convolution_multiply_fusion
  112.2 8.8 %all-reduce = s32[1152]{0:T(1024)S(1)} all-reduce(s32[1152]{0:T(1024)S(1)} %get-tuple-element.4), channel_id=1, replica_groups=mesh['dp'=4,'ctx'=8] {'ctx'}, use_global_device_ids=true, to_apply=%add | all-reduce | flops 1152 | bytes 9216
  121.2 31.3 %all_gather.24 = bf16[1152,256]{1,0:T(8,128)(2,1)S(1)} all-gather(bf16[144,256]{1,0:T(8,128)(2,1)S(1)} %copy-done.5), channel_id=1, replica_groups=mesh['dp'=4,'ctx'=8] {'ctx'}, dimensions={0}, use_global_device_ids=true | all-gather | bytes 663552 | tf_op jit(solution)/shard_map/all_gather | solution.py:106
  152.6 0.6 collective-permute-start.1
  153.2 0.6 copy_bitcast_fusion.3
  153.8 0.7 copy.91
  154.5 1.7 collective-permute-done.1
  156.3 0.3 copy.42
  156.6 26.2 %all-gather = f32[8,144,2]{1,2,0:T(2,128)S(1)} all-gather(f32[1,144,2]{1,2,0:T(2,128)S(1)} %bitcast.99), channel_id=1, replica_groups=mesh['dp'=4,'ctx'=8] {'ctx'}, dimensions={0}, use_global_device_ids=true | all-gather | bytes 10368 | tf_op jit(solution)/shard_map/all_gather | solution.py:102
  183.2 0.4 convolution_bitcast_fusion
  183.6 0.7 fusion.9
  184.3 0.7 copy_bitcast_fusion
  (32 shorter events, 1.1 us)
Async XLA Ops:
  0.6 36.7 %copy-start.1 = (bf16[144,256]{1,0:T(8,128)(2,1)S(1)}, bf16[144,256]{1,0:T(8,128)(2,1)}, u32[]{:S(2)}) copy-start(bf16[144,256]{1,0:T(8,128)(2,1)} %param.5) | copy-start | bytes 221188
  37.8 36.6 %copy-start.6 = (bf16[144,256]{1,0:T(8,128)(2,1)S(1)}, bf16[144,256]{1,0:T(8,128)(2,1)}, u32[]{:S(2)}) copy-start(bf16[144,256]{1,0:T(8,128)(2,1)} %param.7) | copy-start | bytes 221188
  38.3 68.6 %copy-start.4 = (bf16[144,256]{1,0:T(8,128)(2,1)S(1)}, bf16[144,256]{1,0:T(8,128)(2,1)}, u32[]{:S(2)}) copy-start(bf16[144,256]{1,0:T(8,128)(2,1)} %param.8) | copy-start | bytes 221188
  38.3 114.2 %collective-permute-start = (f32[2,144]{1,0:T(2,128)S(1)}, f32[2,144]{1,0:T(2,128)S(1)}, u32[]{:S(2)}, u32[]{:S(2)}) collective-permute-start(f32[2,144]{1,0:T(2,128)S(1)} %get-tuple-element.6), channel_id=1, source_target_pairs={{0,7},{1,0},{2,1},{3,2},{4,3},{5,4},{6,5},{7,6},{8,15},{9,8},{10,9... | collective-permute-start | bytes 3464 | tf_op jit(solution)/shard_map/ppermute | solution.py:19
  106.9 2.9 %copy-start = (bf16[1152,256]{0,1:T(8,128)(2,1)S(1)}, bf16[1152,256]{0,1:T(8,128)(2,1)}, u32[]{:S(2)}) copy-start(bf16[1152,256]{0,1:T(8,128)(2,1)} %copy.31) | copy-start | bytes 1769476
  109.8 2.0 %copy-start.2 = (bf16[144,256]{1,0:T(8,128)(2,1)S(1)}, bf16[144,256]{1,0:T(8,128)(2,1)}, u32[]{:S(2)}) copy-start(bf16[144,256]{1,0:T(8,128)(2,1)} %param.6) | copy-start | bytes 221188
  111.8 9.4 %copy-start.5 = (bf16[144,256]{1,0:T(8,128)(2,1)S(1)}, bf16[144,256]{1,0:T(8,128)(2,1)}, u32[]{:S(2)}) copy-start(bf16[144,256]{1,0:T(8,128)(2,1)} %param.8) | copy-start | bytes 221188
  111.8 41.3 %copy-start.3 = (bf16[144,2,128]{2,0,1:T(8,128)(2,1)S(1)}, bf16[144,2,128]{2,0,1:T(8,128)(2,1)}, u32[]{:S(2)}) copy-start(bf16[144,2,128]{2,0,1:T(8,128)(2,1)} %get-tuple-element.11) | copy-start | bytes 221188
  152.6 3.6 %collective-permute-start.1 = (f32[2,288]{1,0:T(2,128)S(1)}, f32[2,288]{1,0:T(2,128)S(1)}, u32[]{:S(2)}, u32[]{:S(2)}) collective-permute-start(f32[2,288]{1,0:T(2,128)S(1)} %pad_maximum_fusion.1), channel_id=1, source_target_pairs={{0,6},{1,7},{2,0},{3,1},{4,2},{5,3},{6,4},{7,5},{8,14},{9,15},{10,... | collective-permute-start | bytes 6920 | tf_op jit(solution)/shard_map/ppermute | solution.py:19
  156.3 26.7 %collective-permute-start.2 = (f32[2,576]{1,0:T(2,128)S(1)}, f32[2,576]{1,0:T(2,128)S(1)}, u32[]{:S(2)}, u32[]{:S(2)}) collective-permute-start(f32[2,576]{1,0:T(2,128)S(1)} %pad_maximum_fusion), channel_id=1, source_target_pairs={{0,4},{1,5},{2,6},{3,7},{4,0},{5,1},{6,2},{7,3},{8,12},{9,13},{10,... | collective-permute-start | bytes 13832 | tf_op jit(solution)/shard_map/ppermute | solution.py:19
  156.6 27.0 %copy-start.7 = (bf16[144,256]{1,0:T(8,128)(2,1)S(1)}, bf16[144,256]{1,0:T(8,128)(2,1)}, u32[]{:S(2)}) copy-start(bf16[144,256]{1,0:T(8,128)(2,1)} %param.7) | copy-start | bytes 221188
